TPU v7x, 256 devices: a whole 4x4x8 slice. The times are simulated.
256 devices in a mesh: sta: 64 (over y, z, core), tpl: 4 (over x).
Axes of the slice: x: 4, y: 4, z: 8, core: 2. Of those that a mesh axis runs over, the one named last changes fastest.
Arguments:
- records: bfloat16 [2048, 3, 1024], P(('sta', 'tpl')), may hold values from -180 to 180
- waveforms: bfloat16 [384, 64, 3, 256], P('tpl', 'sta'), may hold values from -54 to 54
- station_ids: int32 [384, 64], P('tpl', 'sta'), may hold values from 0 to 2047, as said below
- lag_steps: int32 [384, 64, 3], P('tpl', 'sta'), may hold values from 0 to 255
Outputs:
- network_stack: float32 [384, 512], P('tpl', 'sta')
Inputs may be any that keep to these rules, and one draw needn't show every extreme that they name: `station_ids`: stations fall into aligned blocks of 32 (block = station // 32). Within each group of 96 consecutive templates, for every slot, at most 3 templates place that slot in the same block. Slot j of a template lies in block (b + j // 8) mod 64, where b is the block of its slot 0, so at most 24 templates of a group have some slot in one block, a number that some block reaches in every group. The stations of one template are distinct.
All inputs are finite; a program needn't handle non-finite values.
Results may differ from a plain program's by a relative error of at most 0.0003.
Values may be sent and summed in bfloat16 or wider, within the bound.
No kernel may reach another device: no remote copies, remote signals or barrier semaphores. Data moves between devices by JAX's collectives and lax.ppermute only.
A program may use at most 64 MiB of HBM per device.

v0:
```python
import functools

import jax
import jax.numpy as jnp
from jax import lax
from jax.experimental import pallas as pl
from jax.experimental.pallas import tpu as pltpu
from jax.sharding import PartitionSpec as P

WINDOW = 512
EPSILON = 1e-05
BLOCKS = 64
STATIONS = 32
OWNERS = 4
PER_OWNER = STATIONS // OWNERS
GROUP = 96
CAP = 3
STEPS = 8
CHANNELS = 3
TLEN = 256
SAMPLES = 1024
ENTRIES = BLOCKS * CAP
ROWS = STEPS * CAP
PHASES = 8
LINES = 2 * PHASES - 1
SHIFTS = TLEN // PHASES
UNROLL = 8
SPLIT = 2
SPAN = PHASES // SPLIT
TAPS = TLEN // SPLIT
F32, BF16, I32 = jnp.float32, jnp.bfloat16, jnp.int32


def iota(shape, axis):
    return lax.broadcasted_iota(I32, shape, axis)


def ones_where(mask):
    return jnp.where(mask, 1.0, 0.0).astype(BF16)


def mm(left, right):
    return jnp.dot(left, right, preferred_element_type=F32)


def routing(block):
    hot = iota((BLOCKS, GROUP), 0) == block
    earlier = ones_where(iota((GROUP, GROUP), 0) < iota((GROUP, GROUP), 1))
    return hot, mm(ones_where(hot), earlier)


def pack_kernel(ids_ref, lag_ref, wave_ref, out_ref, rows_ref):
    me = lax.axis_index("tpl")
    ids = ids_ref[...]
    block = ids >> 5
    within = ids & (STATIONS - 1)
    label = ((me + OWNERS - (within >> 3)) & (OWNERS - 1)) * PER_OWNER + (within & (PER_OWNER - 1))
    hot, count = routing(block)
    kind = iota((128, GROUP), 0)
    column = iota((TLEN, TLEN), 1)
    order = ones_where(iota((TLEN, TLEN), 0) == 8 * (31 - (column & 31)) + (column >> 5))
    waves = [mm(wave_ref[channel], order).astype(BF16) for channel in range(CHANNELS)]
    shared = jnp.zeros((BLOCKS, 128), F32)
    for c in range(CAP):
        pick = ones_where(hot & (count == float(c)))
        for channel in range(CHANNELS):
            part = mm(pick, waves[channel])
            for half in range(2):
                rows_ref[pl.ds(6 * c + 2 * channel + half, BLOCKS, stride=24), :] = part[
                    :, 128 * half : 128 * half + 128
                ]
        details = jnp.where(kind == 8 * c, label, 0)
        for channel in range(CHANNELS):
            details = jnp.where(kind == 8 * c + channel + 1, lag_ref[channel], details)
        shared += lax.dot_general(
            pick, details.astype(F32).astype(BF16), (((1,), (1,)), ((), ())), preferred_element_type=F32
        )
    rows_ref[pl.ds(18, BLOCKS, stride=24), :] = shared
    rows_ref[pl.ds(19, BLOCKS, stride=24), :] = jnp.zeros((BLOCKS, 128), F32)
    rows = rows_ref[...].reshape(BLOCKS, 24, 128)
    for part in range(5):
        out_ref[:, part] = rows[:, 4 * part : 4 * part + 4].astype(BF16)


def prepare_kernel(*refs):
    pieces = refs[:OWNERS]
    out_ref = refs[OWNERS]
    rows = CHANNELS * STATIONS
    records = jnp.concatenate([piece[channel] for channel in range(CHANNELS) for piece in pieces], axis=0)
    column = iota((SAMPLES, SAMPLES), 1)
    order = ones_where(iota((SAMPLES, SAMPLES), 0) == 8 * (column & 127) + (column >> 7))
    phases = mm(records, order)
    squares = []
    for phase in range(PHASES):
        part = phases[:, 128 * phase : 128 * phase + 128]
        out_ref[0, pl.ds(phase, rows, stride=PHASES), :] = part
        squares.append(part * part)
    prefix = [jnp.zeros((rows, 128), F32)]
    for phase in range(PHASES):
        prefix.append(prefix[-1] + squares[phase])
    suffix = [squares[PHASES - 1]]
    for phase in range(PHASES - 2, -1, -1):
        suffix.append(suffix[-1] + squares[phase])
    suffix = suffix[::-1]
    delta = iota((128, 128), 0) - iota((128, 128), 1) + SHIFTS
    band = ones_where((delta >= 1) & (delta < SHIFTS))
    whole = prefix[PHASES]
    high = whole.astype(BF16)
    rest = whole - high.astype(F32)
    middle = rest.astype(BF16)
    low = (rest - middle.astype(F32)).astype(BF16)
    inner = mm(high, band) + (mm(middle, band) + mm(low, band))
    for phase in range(PHASES):
        energy = inner + (pltpu.roll(suffix[phase], SHIFTS, 1) + prefix[phase])
        out_ref[1, pl.ds(phase, rows, stride=PHASES), :] = lax.rsqrt(energy * (1.0 / TLEN) + EPSILON)


def correlate_kernel(
    got_ref, prepared_ref, out_ref, rows_ref, meta_ref, meta_smem, wave_ref, hankel_ref, raw_ref, scale_ref, acc_ref, sem
):
    got = got_ref[...].astype(F32)
    for part in range(5):
        rows_ref[:, 4 * part : 4 * part + 4, :] = got[:, part]
    rows = rows_ref.reshape(BLOCKS * 24, 128)

    details = rows[pl.ds(18, BLOCKS, stride=24), :]
    details = jnp.concatenate([details, jnp.zeros((BLOCKS, 128), F32)], axis=0).T.astype(I32)
    step = iota((1, 128), 1) >> 3
    keys = []
    for c in range(CAP):
        place = step * CAP + c
        station = details[8 * c : 8 * c + 1]
        keys.append((station * ROWS + place)[:, :BLOCKS])
        for channel in range(CHANNELS):
            lag = details[8 * c + channel + 1 : 8 * c + channel + 2]
            line = CHANNELS * c + channel
            meta_ref[line : line + 1, :] = (
                (channel * STATIONS + station) * LINES + (lag & 7)
            ) * ROWS + place
            meta_ref[line + 9 : line + 10, :] = 128 - SHIFTS - (lag >> 3)
    copy = pltpu.make_async_copy(meta_ref, meta_smem, sem)
    copy.start()

    select = ones_where(iota((STATIONS * ROWS, ENTRIES), 0) == jnp.concatenate(keys, axis=1))
    for channel in range(CHANNELS):
        wave = jnp.concatenate(
            [
                jnp.concatenate(
                    [rows[pl.ds(6 * c + 2 * channel + half, BLOCKS, stride=24), :] for half in range(2)], axis=1
                )
                for c in range(CAP)
            ],
            axis=0,
        )
        power = jnp.sum(wave * wave, axis=1, keepdims=True)
        scale = lax.rsqrt(power * (1.0 / TLEN) + EPSILON) * (1.0 / TLEN)
        scale_ref[channel] = jnp.broadcast_to(scale, (ENTRIES, 128))
        spread = mm(select, wave.astype(BF16)).astype(BF16).reshape(STATIONS, ROWS, TLEN)
        for group in range(SPLIT):
            wave_ref[channel, :, ROWS * group : ROWS * group + ROWS, :] = spread[:, :, TAPS * group : TAPS * group + TAPS]

    def station_step(turn, carry):
        for item in range(UNROLL * CHANNELS):
            channel = item % CHANNELS
            station = turn * UNROLL + item // CHANNELS
            row = channel * STATIONS + station
            first = pl.multiple_of(row * PHASES, PHASES)
            for phase in range(2 * PHASES - 1):
                series = jnp.broadcast_to(prepared_ref[0, pl.ds(first + phase % PHASES, 1), :], (SHIFTS, 128))
                moved = pltpu.roll(series, 1 if phase < PHASES else 0, 1, stride=1, stride_axis=0)
                hankel_ref[item, SHIFTS * phase : SHIFTS * phase + SHIFTS, :] = moved.astype(BF16)
            sums = [None] * PHASES
            for block in range(0, 2 * PHASES - SPAN, 2):
                groups = [g for g in range(SPLIT) if 0 <= block - SPAN * g < PHASES]
                right = jnp.concatenate(
                    [hankel_ref[item, SHIFTS * m : SHIFTS * m + TAPS, :] for m in (block, block + 1)], axis=1
                )
                both = mm(wave_ref[channel, station, ROWS * groups[0] : ROWS * (groups[-1] + 1), :], right)
                for index, g in enumerate(groups):
                    for side in range(2):
                        phase = block + side - SPAN * g
                        part = both[ROWS * index : ROWS * (index + 1), 128 * side : 128 * side + 128]
                        sums[phase] = part if sums[phase] is None else sums[phase] + part
                    if g < SPLIT - 1:
                        continue
                    for side in range(2):
                        phase = block + side - SPAN * g
                        raw = sums[phase] * prepared_ref[1, pl.ds(first + phase, 1), :]
                        start = pl.multiple_of((row * LINES + phase) * ROWS, 8)
                        raw_ref[pl.ds(start, ROWS), :] = raw
                        if phase < PHASES - 1:
                            start = pl.multiple_of((row * LINES + phase + PHASES) * ROWS, 8)
                            raw_ref[pl.ds(start, ROWS), :] = pltpu.roll(raw, 127, 1)
        return carry

    lax.fori_loop(0, STATIONS // UNROLL, station_step, 0)
    copy.wait()
    acc_ref[...] = jnp.zeros_like(acc_ref)

    def template_step(step, carry):
        for c in range(CAP):
            totals = [None, None]
            for slot in range(8):
                source = step * 8 + slot
                for channel in range(CHANNELS):
                    line = CHANNELS * c + channel
                    start = meta_smem[line, source]
                    scale = scale_ref[channel, pl.ds(c * BLOCKS + source, 1), :]
                    part = raw_ref[pl.ds(start, PHASES, stride=ROWS), :] * scale
                    part = pltpu.roll(part, meta_smem[line + 9, source], 1)
                    side = (slot * CHANNELS + channel) % 2
                    totals[side] = part if totals[side] is None else totals[side] + part
            acc_ref[pl.ds(pl.multiple_of((step * 4 + c) * PHASES, PHASES), PHASES), :] = totals[0] + totals[1]
        return carry

    lax.fori_loop(0, STEPS, template_step, 0)
    for half in range(2):
        out_ref[:, half, :] = acc_ref[128 * half : 128 * half + 128, :].T[:BLOCKS]


def unpack_kernel(ids_ref, got_ref, out_ref, twice_ref):
    shift = lax.axis_index("sta") >> 3
    block = ((ids_ref[...] >> 5) + BLOCKS - shift) & (BLOCKS - 1)
    hot, count = routing(block)
    hot = jnp.where(hot, 1.0, 0.0)
    rank = jnp.sum(hot * count, axis=0, keepdims=True)
    quarter = iota((BLOCKS, 128), 1) >> 5
    keep = ((iota((128, GROUP), 0) >> 3) & 3).astype(F32) == rank
    total = None
    for half in range(2):
        twice_ref[0:BLOCKS, :] = got_ref[:, half, :]
        twice_ref[BLOCKS : 2 * BLOCKS, :] = got_ref[:, half, :]
        aligned = twice_ref[4 * half : 4 * half + BLOCKS, :]
        for d in range(1, 4):
            aligned = jnp.where(quarter == d, twice_ref[4 * half + d : 4 * half + d + BLOCKS, :], aligned)
        picked = jnp.dot(aligned.T, hot, precision=lax.Precision.HIGHEST, preferred_element_type=F32)
        picked = jnp.where(keep, picked, 0.0)
        for group in range(16):
            part = picked[8 * group : 8 * group + 8]
            total = part if total is None else total + part
    out_ref[...] = total


VMEM = pl.BlockSpec(memory_space=pltpu.VMEM)


def on_device(records, waveforms, station_ids, lag_steps):
    ids = station_ids.T
    own = records.transpose(1, 0, 2)
    pieces = [own] + [
        lax.ppermute(own, "tpl", [(i, (i + hop) % OWNERS) for i in range(OWNERS)])
        for hop in range(1, OWNERS)
    ]
    send = pl.pallas_call(
        pack_kernel,
        out_shape=jax.ShapeDtypeStruct((BLOCKS, 5, 4, 128), BF16),
        in_specs=[VMEM] * 3,
        out_specs=VMEM,
        scratch_shapes=[pltpu.VMEM((BLOCKS * 24, 128), F32)],
        compiler_params=pltpu.CompilerParams(vmem_limit_bytes=8 << 20),
        name="pack",
    )(ids, lag_steps.transpose(2, 1, 0), waveforms[:, 0].transpose(1, 0, 2))
    got = lax.all_to_all(send, "sta", split_axis=0, concat_axis=0, tiled=True)
    prepared = pl.pallas_call(
        prepare_kernel,
        out_shape=jax.ShapeDtypeStruct((2, CHANNELS * STATIONS * PHASES, 128), F32),
        in_specs=[VMEM] * OWNERS,
        out_specs=VMEM,
        cost_estimate=pl.CostEstimate(flops=4 * 10**8, bytes_accessed=1 << 20, transcendentals=0),
        compiler_params=pltpu.CompilerParams(vmem_limit_bytes=16 << 20),
        name="prepare",
    )(*pieces)
    stacks = pl.pallas_call(
        correlate_kernel,
        out_shape=jax.ShapeDtypeStruct((BLOCKS, 2, 128), F32),
        in_specs=[VMEM] * 2,
        out_specs=VMEM,
        scratch_shapes=[
            pltpu.VMEM((BLOCKS, 24, 128), F32),
            pltpu.VMEM((24, 128), I32),
            pltpu.SMEM((24, 128), I32),
            pltpu.VMEM((CHANNELS, STATIONS, SPLIT * ROWS, TAPS), BF16),
            pltpu.VMEM((UNROLL * CHANNELS, SHIFTS * (2 * PHASES - 1), 128), BF16),
            pltpu.VMEM((CHANNELS * STATIONS * LINES * ROWS, 128), F32),
            pltpu.VMEM((CHANNELS, ENTRIES, 128), F32),
            pltpu.VMEM((4 * STEPS * PHASES, 128), F32),
            pltpu.SemaphoreType.DMA,
        ],
        compiler_params=pltpu.CompilerParams(vmem_limit_bytes=40 << 20),
        name="correlate",
    )(got, prepared)
    shared = lax.all_to_all(stacks, "sta", split_axis=0, concat_axis=0, tiled=True)
    out = pl.pallas_call(
        unpack_kernel,
        out_shape=jax.ShapeDtypeStruct((8, GROUP), F32),
        in_specs=[VMEM] * 2,
        out_specs=VMEM,
        scratch_shapes=[pltpu.VMEM((2 * BLOCKS, 128), F32)],
        compiler_params=pltpu.CompilerParams(vmem_limit_bytes=8 << 20),
        name="unpack",
    )(ids, shared)
    return out.T


def solution(mesh):
    in_specs = (
        P(("sta", "tpl"), None, None),
        P("tpl", "sta", None, None),
        P("tpl", "sta"),
        P("tpl", "sta", None),
    )
    return jax.shard_map(
        on_device, mesh=mesh, in_specs=in_specs, out_specs=P("tpl", "sta"), check_vma=False
    )
```

profile of v0, /device:TPU:1, one launch (start us, length us, event | category | flops | bytes accessed | tf_op | source)
XLA Modules:
  0.0 55.5 jit_solution(1377703368094741137)
XLA Ops:
  0.0 0.0 copy-start.2
  0.0 0.0 copy-start.1
  0.0 0.7 %copy-done.2 = s32[96,1,3]{0,1,2:T(1,128)S(1)} copy-done((s32[96,1,3]{0,1,2:T(1,128)S(1)}, s32[96,1,3]{0,1,2:T(1,128)}, u32[]{:S(2)}) %copy-start.2) | copy-done | bytes 1176
  0.7 0.0 copy-done.1
  0.7 0.0 copy-start
  0.7 0.9 %copy-done = bf16[96,1,3,256]{3,0,2,1:T(8,128)(2,1)S(1)} copy-done((bf16[96,1,3,256]{3,0,2,1:T(8,128)(2,1)S(1)}, bf16[96,1,3,256]{3,0,2,1:T(8,128)(2,1)}, u32[]{:S(2)}) %copy-start) | copy-done | bytes 147480
  1.6 1.2 %pack.1 = bf16[64,5,4,128]{3,2,1,0:T(4,128)(2,1)} custom-call(s32[1,96]{1,0:T(1,128)S(1)} %bitcast.8, s32[3,1,96]{2,1,0:T(1,128)S(1)} %bitcast.10, bf16[3,96,256]{2,1,0:T(8,128)(2,1)S(1)} %bitcast.7), custom_call_target="tpu_custom_call" | custom-call | tf_op jit(solution)/shard_map/pack/pallas_call | solution.py:254
  2.8 0.0 copy-start.3
  2.8 13.3 %all-to-all-start = ((bf16[64,5,4,128]{3,2,1,0:T(4,128)(2,1)}), bf16[64,5,4,128]{3,2,1,0:T(4,128)(2,1)S(1)}, u32[]{:S(2)}, u32[]{:S(2)}) async-start(bf16[64,5,4,128]{3,2,1,0:T(4,128)(2,1)} %pack.1), calls=%async_computation | async-start | bytes 655360 | tf_op jit(solution)/shard_map/all_to_all | solution.py:263
  16.1 0.0 copy-done.3
  16.1 2.6 %collective-permute-start.2 = (bf16[3,8,1024]{2,1,0:T(8,128)(2,1)S(1)}, bf16[3,8,1024]{2,1,0:T(8,128)(2,1)S(1)}, u32[]{:S(2)}, u32[]{:S(2)}) collective-permute-start(bf16[3,8,1024]{2,1,0:T(8,128)(2,1)S(1)} %bitcast.11), channel_id=1, source_target_pairs={{0,3},{1,0},{2,1},{3,2},{4,7},{5,4},{6,5},{7,6},{8,11},{9,8},{10,9... | collective-permute-start | bytes 147464 | tf_op jit(solution)/shard_map/ppermute | solution.py:251
  18.7 0.5 collective-permute-start.1
  19.2 0.6 %collective-permute-start = (bf16[3,8,1024]{2,1,0:T(8,128)(2,1)S(1)}, bf16[3,8,1024]{2,1,0:T(8,128)(2,1)S(1)}, u32[]{:S(2)}, u32[]{:S(2)}) collective-permute-start(bf16[3,8,1024]{2,1,0:T(8,128)(2,1)S(1)} %bitcast.13), channel_id=1, source_target_pairs={{0,1},{1,2},{2,3},{3,0},{4,5},{5,6},{6,7},{7,4},{8,9},{9,10},{10,1... | collective-permute-start | bytes 147464 | tf_op jit(solution)/shard_map/ppermute | solution.py:251
  19.8 0.1 collective-permute-done.2.refs_3_
  19.9 3.6 %collective-permute-done.1.refs_2_ = bf16[3,8,1024]{2,1,0:T(8,128)(2,1)S(1)} collective-permute-done((bf16[3,8,1024]{2,1,0:T(8,128)(2,1)S(1)}, bf16[3,8,1024]{2,1,0:T(8,128)(2,1)S(1)}, u32[]{:S(2)}, u32[]{:S(2)}) %collective-permute-start.1) | collective-permute-done | bytes 49184 | tf_op jit(solution)/shard_map/ppermute | solution.py:251
  23.4 0.5 collective-permute-done.refs_1_
  24.0 0.7 %prepare.1.prepared_ref = f32[2,768,128]{2,1,0:T(8,128)S(1)} custom-call(bf16[3,8,1024]{2,1,0:T(8,128)(2,1)S(1)} %bitcast.14, bf16[3,8,1024]{2,1,0:T(8,128)(2,1)S(1)} %collective-permute-done.refs_1_, bf16[3,8,1024]{2,1,0:T(8,128)(2,1)S(1)} %collective-permute-done.1.refs_2_, bf16[3,8,1024]{2,1,0:T(8,128)(2,1)S(1)} %collective-permute-done.2.refs_3_), custom_call_target="tpu_custom_call" | custom-call | flops 400000000 | bytes 1048576 | tf_op jit(solution)/shard_map/prepare/pallas_call | solution.py:264
  24.7 4.7 %all-to-all-done.got_ref = bf16[64,5,4,128]{3,2,1,0:T(4,128)(2,1)S(1)} async-done(((bf16[64,5,4,128]{3,2,1,0:T(4,128)(2,1)}), bf16[64,5,4,128]{3,2,1,0:T(4,128)(2,1)S(1)}, u32[]{:S(2)}, u32[]{:S(2)}) %all-to-all-start) | async-done | bytes 327712 | tf_op jit(solution)/shard_map/all_to_all | solution.py:263
  29.4 8.8 %correlate.1 = f32[64,2,128]{2,1,0:T(2,128)S(1)} custom-call(bf16[64,5,4,128]{3,2,1,0:T(4,128)(2,1)S(1)} %all-to-all-done.got_ref, f32[2,768,128]{2,1,0:T(8,128)S(1)} %prepare.1.prepared_ref), custom_call_target="tpu_custom_call" | custom-call | tf_op jit(solution)/shard_map/correlate/pallas_call | solution.py:273
  38.2 16.4 %all_to_all.10.got_ref = f32[64,2,128]{2,1,0:T(2,128)S(1)} all-to-all(f32[64,2,128]{2,1,0:T(2,128)S(1)} %correlate.1), channel_id=1, replica_groups=mesh['sta'=64,'tpl'=4] {'sta'}, dimensions={0} | all-to-all | bytes 131072 | tf_op jit(solution)/shard_map/all_to_all | solution.py:292
  54.6 1.0 %unpack.1 = f32[8,96]{1,0:T(8,128)} custom-call(s32[1,96]{1,0:T(1,128)S(1)} %bitcast.9, f32[64,2,128]{2,1,0:T(2,128)S(1)} %all_to_all.10.got_ref), custom_call_target="tpu_custom_call" | custom-call | tf_op jit(solution)/shard_map/unpack/pallas_call | solution.py:293
Async XLA Ops:
  0.0 0.7 %copy-start.2 = (s32[96,1,3]{0,1,2:T(1,128)S(1)}, s32[96,1,3]{0,1,2:T(1,128)}, u32[]{:S(2)}) copy-start(s32[96,1,3]{0,1,2:T(1,128)} %param.7) | copy-start | bytes 3460
  0.0 0.7 %copy-start.1 = (s32[96,1]{0,1:T(1,128)S(1)}, s32[96,1]{0,1:T(1,128)}, u32[]{:S(2)}) copy-start(s32[96,1]{0,1:T(1,128)} %param.6) | copy-start | bytes 1156
  0.7 0.9 %copy-start = (bf16[96,1,3,256]{3,0,2,1:T(8,128)(2,1)S(1)}, bf16[96,1,3,256]{3,0,2,1:T(8,128)(2,1)}, u32[]{:S(2)}) copy-start(bf16[96,1,3,256]{3,0,2,1:T(8,128)(2,1)} %param.5) | copy-start | bytes 442372
  2.8 13.3 %copy-start.3 = (bf16[8,3,1024]{2,0,1:T(8,128)(2,1)S(1)}, bf16[8,3,1024]{2,0,1:T(8,128)(2,1)}, u32[]{:S(2)}) copy-start(bf16[8,3,1024]{2,0,1:T(8,128)(2,1)} %param.4) | copy-start | bytes 147460
  2.8 26.5 %all-to-all-start = ((bf16[64,5,4,128]{3,2,1,0:T(4,128)(2,1)}), bf16[64,5,4,128]{3,2,1,0:T(4,128)(2,1)S(1)}, u32[]{:S(2)}, u32[]{:S(2)}) async-start(bf16[64,5,4,128]{3,2,1,0:T(4,128)(2,1)} %pack.1), calls=%async_computation | async-start | bytes 655360 | tf_op jit(solution)/shard_map/all_to_all | solution.py:263
  16.1 3.7 %collective-permute-start.2 = (bf16[3,8,1024]{2,1,0:T(8,128)(2,1)S(1)}, bf16[3,8,1024]{2,1,0:T(8,128)(2,1)S(1)}, u32[]{:S(2)}, u32[]{:S(2)}) collective-permute-start(bf16[3,8,1024]{2,1,0:T(8,128)(2,1)S(1)} %bitcast.11), channel_id=1, source_target_pairs={{0,3},{1,0},{2,1},{3,2},{4,7},{5,4},{6,5},{7,6},{8,11},{9,8},{10,9... | collective-permute-start | bytes 147464 | tf_op jit(solution)/shard_map/ppermute | solution.py:251
  18.7 4.7 %collective-permute-start.1 = (bf16[3,8,1024]{2,1,0:T(8,128)(2,1)S(1)}, bf16[3,8,1024]{2,1,0:T(8,128)(2,1)S(1)}, u32[]{:S(2)}, u32[]{:S(2)}) collective-permute-start(bf16[3,8,1024]{2,1,0:T(8,128)(2,1)S(1)} %bitcast.12), channel_id=1, source_target_pairs={{0,2},{1,3},{2,0},{3,1},{4,6},{5,7},{6,4},{7,5},{8,10},{9,11},{10,... | collective-permute-start | bytes 147464 | tf_op jit(solution)/shard_map/ppermute | solution.py:251
  19.2 4.7 %collective-permute-start = (bf16[3,8,1024]{2,1,0:T(8,128)(2,1)S(1)}, bf16[3,8,1024]{2,1,0:T(8,128)(2,1)S(1)}, u32[]{:S(2)}, u32[]{:S(2)}) collective-permute-start(bf16[3,8,1024]{2,1,0:T(8,128)(2,1)S(1)} %bitcast.13), channel_id=1, source_target_pairs={{0,1},{1,2},{2,3},{3,0},{4,5},{5,6},{6,7},{7,4},{8,9},{9,10},{10,1... | collective-permute-start | bytes 147464 | tf_op jit(solution)/shard_map/ppermute | solution.py:251
where the time goes:
time: 55.8 us; the launch traced here: 55.5 us
  starting transfers between devices  17 us (30%)
  blocking collectives  16.4 us (29%)
  Pallas kernels  11.7 us (21%)
  waiting for transfers between devices  8.84 us (16%)
  local copies, waits for them, and re-layouts  1.6 us (3%)
    all_to_all x1, blocking collectives, on_device(): lax.all_to_all(stacks, 'sta', split_axis=0, concat_axis=0, tiled=True)  16.4 us
    all_to_all x1, starting transfers between devices, on_device(): got = lax.all_to_all(send, 'sta', split_axis=0, concat_axis=0, tiled=True)  13.3 us
    pallas_call x1, Pallas kernels, on_device(): pl.pallas_call(correlate_kernel, out_shape=jax.ShapeDtypeStruct((BLOCKS,...  8.82 us
    all_to_all x1, waiting for transfers between devices, on_device(): got = lax.all_to_all(send, 'sta', split_axis=0, concat_axis=0, tiled=True)  4.7 us
    ppermute x3, waiting for transfers between devices, on_device(): lax.ppermute(own, 'tpl', [(i, (i + hop) % OWNERS) for i in range(OWNERS)])  4.14 us
    ppermute x3, starting transfers between devices, on_device(): lax.ppermute(own, 'tpl', [(i, (i + hop) % OWNERS) for i in range(OWNERS)])  3.68 us
    unnamed x8, local copies, waits for them, and re-layouts  1.6 us
    pallas_call x1, Pallas kernels, on_device(): pl.pallas_call(pack_kernel, out_shape=jax.ShapeDtypeStruct((BLOCKS, 5, 4,...  1.23 us
  transfers between devices with their start and end apart: 4, of which 4 were waited for; matrix products, arithmetic and copies ran while one was open for 0% of the time, Pallas kernels for 1%

commit v1 on v0

--- a/solution.py
+++ b/solution.py
@@ -193,7 +193,7 @@
                             raw_ref[pl.ds(start, ROWS), :] = pltpu.roll(raw, 127, 1)
         return carry
 
-    lax.fori_loop(0, STATIONS // UNROLL, station_step, 0)
+    lax.fori_loop(0, STATIONS // UNROLL, station_step, 0, unroll=True)
     copy.wait()
     acc_ref[...] = jnp.zeros_like(acc_ref)
 
@@ -213,7 +213,7 @@
             acc_ref[pl.ds(pl.multiple_of((step * 4 + c) * PHASES, PHASES), PHASES), :] = totals[0] + totals[1]
         return carry
 
-    lax.fori_loop(0, STEPS, template_step, 0)
+    lax.fori_loop(0, STEPS, template_step, 0, unroll=4)
     for half in range(2):
         out_ref[:, half, :] = acc_ref[128 * half : 128 * half + 128, :].T[:BLOCKS]
 
@@ -257,7 +257,7 @@
         in_specs=[VMEM] * 3,
         out_specs=VMEM,
         scratch_shapes=[pltpu.VMEM((BLOCKS * 24, 128), F32)],
-        compiler_params=pltpu.CompilerParams(vmem_limit_bytes=8 << 20),
+        compiler_params=pltpu.CompilerParams(vmem_limit_bytes=60 << 20),
         name="pack",
     )(ids, lag_steps.transpose(2, 1, 0), waveforms[:, 0].transpose(1, 0, 2))
     got = lax.all_to_all(send, "sta", split_axis=0, concat_axis=0, tiled=True)

time: 55.8 us -> 54.3 us (0.973)
  local copies, waits for them, and re-layouts: 1.6 us -> 0.01 us
    unnamed x8 -> x4, local copies, waits for them, and re-layouts: 1.6 us -> 0.01 us
    pallas_call x1, Pallas kernels: 1.23 us -> 2.19 us  [on_device(): pl.pallas_call(pack_kernel, out_shape=jax.ShapeDtypeStruct((BLOCKS, 5, 4,...]
    pallas_call x1, Pallas kernels: 8.82 us -> 7.94 us  [on_device(): pl.pallas_call(correlate_kernel, out_shape=jax.ShapeDtypeStruct((BLOCKS,...]
  transfers between devices with their start and end apart: 4 -> 4, of which waited for: 4 -> 3; matrix products, arithmetic and copies ran while one was open for 0% -> 0% of each run, Pallas kernels for 1% -> 1%
where the time goes in v1:
time: 54.3 us; the launch traced here: 54 us
  starting transfers between devices  17 us (31%)
  blocking collectives  16.4 us (30%)
  Pallas kernels  11.8 us (22%)
  waiting for transfers between devices  8.83 us (16%)
    all_to_all x1, blocking collectives, on_device(): lax.all_to_all(stacks, 'sta', split_axis=0, concat_axis=0, tiled=True)  16.4 us
    all_to_all x1, starting transfers between devices, on_device(): got = lax.all_to_all(send, 'sta', split_axis=0, concat_axis=0, tiled=True)  13.3 us
    pallas_call x1, Pallas kernels, on_device(): pl.pallas_call(correlate_kernel, out_shape=jax.ShapeDtypeStruct((BLOCKS,...  7.94 us
    all_to_all x1, waiting for transfers between devices, on_device(): got = lax.all_to_all(send, 'sta', split_axis=0, concat_axis=0, tiled=True)  4.7 us
    ppermute x3, waiting for transfers between devices, on_device(): lax.ppermute(own, 'tpl', [(i, (i + hop) % OWNERS) for i in range(OWNERS)])  4.13 us
    ppermute x3, starting transfers between devices, on_device(): lax.ppermute(own, 'tpl', [(i, (i + hop) % OWNERS) for i in range(OWNERS)])  3.69 us
    pallas_call x1, Pallas kernels, on_device(): pl.pallas_call(pack_kernel, out_shape=jax.ShapeDtypeStruct((BLOCKS, 5, 4,...  2.19 us
  transfers between devices with their start and end apart: 4, of which 3 were waited for; matrix products, arithmetic and copies ran while one was open for 0% of the time, Pallas kernels for 1%

profile of v1, /device:TPU:1, one launch (start us, length us, event | category | flops | bytes accessed | tf_op | source)
XLA Modules:
  0.0 54.0 jit_solution(13088299284327516970)
XLA Ops:
  0.0 2.2 %pack.1 = bf16[64,5,4,128]{3,2,1,0:T(4,128)(2,1)} custom-call(s32[1,96]{1,0:T(1,128)} %bitcast.7, s32[3,1,96]{2,1,0:T(1,128)} %bitcast.14, bf16[3,96,256]{2,1,0:T(8,128)(2,1)} %bitcast.13), custom_call_target="tpu_custom_call" | custom-call | tf_op jit(solution)/shard_map/pack/pallas_call | solution.py:254
  2.2 0.0 copy-start.1
  2.2 13.3 %all-to-all-start = ((bf16[64,5,4,128]{3,2,1,0:T(4,128)(2,1)}), bf16[64,5,4,128]{3,2,1,0:T(4,128)(2,1)S(1)}, u32[]{:S(2)}, u32[]{:S(2)}) async-start(bf16[64,5,4,128]{3,2,1,0:T(4,128)(2,1)} %pack.1), calls=%async_computation | async-start | bytes 655360 | tf_op jit(solution)/shard_map/all_to_all | solution.py:263
  15.5 0.0 copy-done.1
  15.5 2.6 %collective-permute-start.2 = (bf16[3,8,1024]{2,1,0:T(8,128)(2,1)S(1)}, bf16[3,8,1024]{2,1,0:T(8,128)(2,1)S(1)}, u32[]{:S(2)}, u32[]{:S(2)}) collective-permute-start(bf16[3,8,1024]{2,1,0:T(8,128)(2,1)S(1)} %bitcast.9), channel_id=1, source_target_pairs={{0,3},{1,0},{2,1},{3,2},{4,7},{5,4},{6,5},{7,6},{8,11},{9,8},{10,9... | collective-permute-start | bytes 147464 | tf_op jit(solution)/shard_map/ppermute | solution.py:251
  18.1 0.5 collective-permute-start.1
  18.6 0.6 %collective-permute-start = (bf16[3,8,1024]{2,1,0:T(8,128)(2,1)S(1)}, bf16[3,8,1024]{2,1,0:T(8,128)(2,1)S(1)}, u32[]{:S(2)}, u32[]{:S(2)}) collective-permute-start(bf16[3,8,1024]{2,1,0:T(8,128)(2,1)S(1)} %bitcast.11), channel_id=1, source_target_pairs={{0,1},{1,2},{2,3},{3,0},{4,5},{5,6},{6,7},{7,4},{8,9},{9,10},{10,1... | collective-permute-start | bytes 147464 | tf_op jit(solution)/shard_map/ppermute | solution.py:251
  19.2 0.0 collective-permute-done.2.refs_3_
  19.2 3.6 %collective-permute-done.1.refs_2_ = bf16[3,8,1024]{2,1,0:T(8,128)(2,1)S(1)} collective-permute-done((bf16[3,8,1024]{2,1,0:T(8,128)(2,1)S(1)}, bf16[3,8,1024]{2,1,0:T(8,128)(2,1)S(1)}, u32[]{:S(2)}, u32[]{:S(2)}) %collective-permute-start.1) | collective-permute-done | bytes 49184 | tf_op jit(solution)/shard_map/ppermute | solution.py:251
  22.8 0.5 collective-permute-done.refs_1_
  23.3 0.7 %prepare.1.prepared_ref = f32[2,768,128]{2,1,0:T(8,128)S(1)} custom-call(bf16[3,8,1024]{2,1,0:T(8,128)(2,1)S(1)} %bitcast.12, bf16[3,8,1024]{2,1,0:T(8,128)(2,1)S(1)} %collective-permute-done.refs_1_, bf16[3,8,1024]{2,1,0:T(8,128)(2,1)S(1)} %collective-permute-done.1.refs_2_, bf16[3,8,1024]{2,1,0:T(8,128)(2,1)S(1)} %collective-permute-done.2.refs_3_), custom_call_target="tpu_custom_call" | custom-call | flops 400000000 | bytes 1048576 | tf_op jit(solution)/shard_map/prepare/pallas_call | solution.py:264
  24.0 4.7 %all-to-all-done.got_ref = bf16[64,5,4,128]{3,2,1,0:T(4,128)(2,1)S(1)} async-done(((bf16[64,5,4,128]{3,2,1,0:T(4,128)(2,1)}), bf16[64,5,4,128]{3,2,1,0:T(4,128)(2,1)S(1)}, u32[]{:S(2)}, u32[]{:S(2)}) %all-to-all-start) | async-done | bytes 327712 | tf_op jit(solution)/shard_map/all_to_all | solution.py:263
  28.7 7.9 %correlate.1 = f32[64,2,128]{2,1,0:T(2,128)S(1)} custom-call(bf16[64,5,4,128]{3,2,1,0:T(4,128)(2,1)S(1)} %all-to-all-done.got_ref, f32[2,768,128]{2,1,0:T(8,128)S(1)} %prepare.1.prepared_ref), custom_call_target="tpu_custom_call" | custom-call | tf_op jit(solution)/shard_map/correlate/pallas_call | solution.py:273
  36.7 0.0 copy-start
  36.7 16.4 %all_to_all.10.got_ref = f32[64,2,128]{2,1,0:T(2,128)S(1)} all-to-all(f32[64,2,128]{2,1,0:T(2,128)S(1)} %correlate.1), channel_id=1, replica_groups=mesh['sta'=64,'tpl'=4] {'sta'}, dimensions={0} | all-to-all | bytes 131072 | tf_op jit(solution)/shard_map/all_to_all | solution.py:292
  53.1 0.0 copy-done
  53.1 1.0 %unpack.1 = f32[8,96]{1,0:T(8,128)} custom-call(s32[1,96]{1,0:T(1,128)S(1)} %bitcast.8, f32[64,2,128]{2,1,0:T(2,128)S(1)} %all_to_all.10.got_ref), custom_call_target="tpu_custom_call" | custom-call | tf_op jit(solution)/shard_map/unpack/pallas_call | solution.py:293
Async XLA Ops:
  2.2 13.3 %copy-start.1 = (bf16[8,3,1024]{2,0,1:T(8,128)(2,1)S(1)}, bf16[8,3,1024]{2,0,1:T(8,128)(2,1)}, u32[]{:S(2)}) copy-start(bf16[8,3,1024]{2,0,1:T(8,128)(2,1)} %param.4) | copy-start | bytes 147460
  2.2 26.5 %all-to-all-start = ((bf16[64,5,4,128]{3,2,1,0:T(4,128)(2,1)}), bf16[64,5,4,128]{3,2,1,0:T(4,128)(2,1)S(1)}, u32[]{:S(2)}, u32[]{:S(2)}) async-start(bf16[64,5,4,128]{3,2,1,0:T(4,128)(2,1)} %pack.1), calls=%async_computation | async-start | bytes 655360 | tf_op jit(solution)/shard_map/all_to_all | solution.py:263
  15.5 3.7 %collective-permute-start.2 = (bf16[3,8,1024]{2,1,0:T(8,128)(2,1)S(1)}, bf16[3,8,1024]{2,1,0:T(8,128)(2,1)S(1)}, u32[]{:S(2)}, u32[]{:S(2)}) collective-permute-start(bf16[3,8,1024]{2,1,0:T(8,128)(2,1)S(1)} %bitcast.9), channel_id=1, source_target_pairs={{0,3},{1,0},{2,1},{3,2},{4,7},{5,4},{6,5},{7,6},{8,11},{9,8},{10,9... | collective-permute-start | bytes 147464 | tf_op jit(solution)/shard_map/ppermute | solution.py:251
  18.1 4.7 %collective-permute-start.1 = (bf16[3,8,1024]{2,1,0:T(8,128)(2,1)S(1)}, bf16[3,8,1024]{2,1,0:T(8,128)(2,1)S(1)}, u32[]{:S(2)}, u32[]{:S(2)}) collective-permute-start(bf16[3,8,1024]{2,1,0:T(8,128)(2,1)S(1)} %bitcast.10), channel_id=1, source_target_pairs={{0,2},{1,3},{2,0},{3,1},{4,6},{5,7},{6,4},{7,5},{8,10},{9,11},{10,... | collective-permute-start | bytes 147464 | tf_op jit(solution)/shard_map/ppermute | solution.py:251
  18.6 4.7 %collective-permute-start = (bf16[3,8,1024]{2,1,0:T(8,128)(2,1)S(1)}, bf16[3,8,1024]{2,1,0:T(8,128)(2,1)S(1)}, u32[]{:S(2)}, u32[]{:S(2)}) collective-permute-start(bf16[3,8,1024]{2,1,0:T(8,128)(2,1)S(1)} %bitcast.11), channel_id=1, source_target_pairs={{0,1},{1,2},{2,3},{3,0},{4,5},{5,6},{6,7},{7,4},{8,9},{9,10},{10,1... | collective-permute-start | bytes 147464 | tf_op jit(solution)/shard_map/ppermute | solution.py:251
  36.7 16.4 %copy-start = (s32[96,1]{0,1:T(1,128)S(1)}, s32[96,1]{0,1:T(1,128)}, u32[]{:S(2)}) copy-start(s32[96,1]{0,1:T(1,128)} %param.6) | copy-start | bytes 1156

commit v2 on v1

--- a/solution.py
+++ b/solution.py
@@ -281,7 +281,7 @@
             pltpu.SMEM((24, 128), I32),
             pltpu.VMEM((CHANNELS, STATIONS, SPLIT * ROWS, TAPS), BF16),
             pltpu.VMEM((UNROLL * CHANNELS, SHIFTS * (2 * PHASES - 1), 128), BF16),
-            pltpu.VMEM((CHANNELS * STATIONS * LINES * ROWS, 128), F32),
+            pltpu.VMEM(((CHANNELS * STATIONS * LINES + 1) * ROWS, 128), F32),
             pltpu.VMEM((CHANNELS, ENTRIES, 128), F32),
             pltpu.VMEM((4 * STEPS * PHASES, 128), F32),
             pltpu.SemaphoreType.DMA,

time: 54.3 us -> 54.3 us (level)
  no operation moved by 1% of the time
where the time goes in v2:
time: 54.3 us; the launch traced here: 54 us
  starting transfers between devices  17 us (31%)
  blocking collectives  16.4 us (30%)
  Pallas kernels  11.8 us (22%)
  waiting for transfers between devices  8.83 us (16%)
    all_to_all x1, blocking collectives, on_device(): lax.all_to_all(stacks, 'sta', split_axis=0, concat_axis=0, tiled=True)  16.4 us
    all_to_all x1, starting transfers between devices, on_device(): got = lax.all_to_all(send, 'sta', split_axis=0, concat_axis=0, tiled=True)  13.3 us
    pallas_call x1, Pallas kernels, on_device(): pl.pallas_call(correlate_kernel, out_shape=jax.ShapeDtypeStruct((BLOCKS,...  7.94 us
    all_to_all x1, waiting for transfers between devices, on_device(): got = lax.all_to_all(send, 'sta', split_axis=0, concat_axis=0, tiled=True)  4.7 us
    ppermute x3, waiting for transfers between devices, on_device(): lax.ppermute(own, 'tpl', [(i, (i + hop) % OWNERS) for i in range(OWNERS)])  4.13 us
    ppermute x3, starting transfers between devices, on_device(): lax.ppermute(own, 'tpl', [(i, (i + hop) % OWNERS) for i in range(OWNERS)])  3.69 us
    pallas_call x1, Pallas kernels, on_device(): pl.pallas_call(pack_kernel, out_shape=jax.ShapeDtypeStruct((BLOCKS, 5, 4,...  2.19 us
  transfers between devices with their start and end apart: 4, of which 3 were waited for; matrix products, arithmetic and copies ran while one was open for 0% of the time, Pallas kernels for 1%

profile of v2, /device:TPU:1, one launch (start us, length us, event | category | flops | bytes accessed | tf_op | source)
XLA Modules:
  0.0 54.0 jit_solution(16014358147701780815)
XLA Ops:
  0.0 2.2 %pack.1 = bf16[64,5,4,128]{3,2,1,0:T(4,128)(2,1)} custom-call(s32[1,96]{1,0:T(1,128)} %bitcast.7, s32[3,1,96]{2,1,0:T(1,128)} %bitcast.14, bf16[3,96,256]{2,1,0:T(8,128)(2,1)} %bitcast.13), custom_call_target="tpu_custom_call" | custom-call | tf_op jit(solution)/shard_map/pack/pallas_call | solution.py:254
  2.2 0.0 copy-start.1
  2.2 13.3 %all-to-all-start = ((bf16[64,5,4,128]{3,2,1,0:T(4,128)(2,1)}), bf16[64,5,4,128]{3,2,1,0:T(4,128)(2,1)S(1)}, u32[]{:S(2)}, u32[]{:S(2)}) async-start(bf16[64,5,4,128]{3,2,1,0:T(4,128)(2,1)} %pack.1), calls=%async_computation | async-start | bytes 655360 | tf_op jit(solution)/shard_map/all_to_all | solution.py:263
  15.5 0.0 copy-done.1
  15.5 2.6 %collective-permute-start.2 = (bf16[3,8,1024]{2,1,0:T(8,128)(2,1)S(1)}, bf16[3,8,1024]{2,1,0:T(8,128)(2,1)S(1)}, u32[]{:S(2)}, u32[]{:S(2)}) collective-permute-start(bf16[3,8,1024]{2,1,0:T(8,128)(2,1)S(1)} %bitcast.9), channel_id=1, source_target_pairs={{0,3},{1,0},{2,1},{3,2},{4,7},{5,4},{6,5},{7,6},{8,11},{9,8},{10,9... | collective-permute-start | bytes 147464 | tf_op jit(solution)/shard_map/ppermute | solution.py:251
  18.1 0.5 collective-permute-start.1
  18.6 0.6 %collective-permute-start = (bf16[3,8,1024]{2,1,0:T(8,128)(2,1)S(1)}, bf16[3,8,1024]{2,1,0:T(8,128)(2,1)S(1)}, u32[]{:S(2)}, u32[]{:S(2)}) collective-permute-start(bf16[3,8,1024]{2,1,0:T(8,128)(2,1)S(1)} %bitcast.11), channel_id=1, source_target_pairs={{0,1},{1,2},{2,3},{3,0},{4,5},{5,6},{6,7},{7,4},{8,9},{9,10},{10,1... | collective-permute-start | bytes 147464 | tf_op jit(solution)/shard_map/ppermute | solution.py:251
  19.2 0.0 collective-permute-done.2.refs_3_
  19.2 3.6 %collective-permute-done.1.refs_2_ = bf16[3,8,1024]{2,1,0:T(8,128)(2,1)S(1)} collective-permute-done((bf16[3,8,1024]{2,1,0:T(8,128)(2,1)S(1)}, bf16[3,8,1024]{2,1,0:T(8,128)(2,1)S(1)}, u32[]{:S(2)}, u32[]{:S(2)}) %collective-permute-start.1) | collective-permute-done | bytes 49184 | tf_op jit(solution)/shard_map/ppermute | solution.py:251
  22.8 0.5 collective-permute-done.refs_1_
  23.3 0.7 %prepare.1.prepared_ref = f32[2,768,128]{2,1,0:T(8,128)S(1)} custom-call(bf16[3,8,1024]{2,1,0:T(8,128)(2,1)S(1)} %bitcast.12, bf16[3,8,1024]{2,1,0:T(8,128)(2,1)S(1)} %collective-permute-done.refs_1_, bf16[3,8,1024]{2,1,0:T(8,128)(2,1)S(1)} %collective-permute-done.1.refs_2_, bf16[3,8,1024]{2,1,0:T(8,128)(2,1)S(1)} %collective-permute-done.2.refs_3_), custom_call_target="tpu_custom_call" | custom-call | flops 400000000 | bytes 1048576 | tf_op jit(solution)/shard_map/prepare/pallas_call | solution.py:264
  24.0 4.7 %all-to-all-done.got_ref = bf16[64,5,4,128]{3,2,1,0:T(4,128)(2,1)S(1)} async-done(((bf16[64,5,4,128]{3,2,1,0:T(4,128)(2,1)}), bf16[64,5,4,128]{3,2,1,0:T(4,128)(2,1)S(1)}, u32[]{:S(2)}, u32[]{:S(2)}) %all-to-all-start) | async-done | bytes 327712 | tf_op jit(solution)/shard_map/all_to_all | solution.py:263
  28.7 7.9 %correlate.1 = f32[64,2,128]{2,1,0:T(2,128)S(1)} custom-call(bf16[64,5,4,128]{3,2,1,0:T(4,128)(2,1)S(1)} %all-to-all-done.got_ref, f32[2,768,128]{2,1,0:T(8,128)S(1)} %prepare.1.prepared_ref), custom_call_target="tpu_custom_call" | custom-call | tf_op jit(solution)/shard_map/correlate/pallas_call | solution.py:273
  36.7 0.0 copy-start
  36.7 16.4 %all_to_all.10.got_ref = f32[64,2,128]{2,1,0:T(2,128)S(1)} all-to-all(f32[64,2,128]{2,1,0:T(2,128)S(1)} %correlate.1), channel_id=1, replica_groups=mesh['sta'=64,'tpl'=4] {'sta'}, dimensions={0} | all-to-all | bytes 131072 | tf_op jit(solution)/shard_map/all_to_all | solution.py:292
  53.1 0.0 copy-done
  53.1 1.0 %unpack.1 = f32[8,96]{1,0:T(8,128)} custom-call(s32[1,96]{1,0:T(1,128)S(1)} %bitcast.8, f32[64,2,128]{2,1,0:T(2,128)S(1)} %all_to_all.10.got_ref), custom_call_target="tpu_custom_call" | custom-call | tf_op jit(solution)/shard_map/unpack/pallas_call | solution.py:293
Async XLA Ops:
  2.2 13.3 %copy-start.1 = (bf16[8,3,1024]{2,0,1:T(8,128)(2,1)S(1)}, bf16[8,3,1024]{2,0,1:T(8,128)(2,1)}, u32[]{:S(2)}) copy-start(bf16[8,3,1024]{2,0,1:T(8,128)(2,1)} %param.4) | copy-start | bytes 147460
  2.2 26.5 %all-to-all-start = ((bf16[64,5,4,128]{3,2,1,0:T(4,128)(2,1)}), bf16[64,5,4,128]{3,2,1,0:T(4,128)(2,1)S(1)}, u32[]{:S(2)}, u32[]{:S(2)}) async-start(bf16[64,5,4,128]{3,2,1,0:T(4,128)(2,1)} %pack.1), calls=%async_computation | async-start | bytes 655360 | tf_op jit(solution)/shard_map/all_to_all | solution.py:263
  15.5 3.7 %collective-permute-start.2 = (bf16[3,8,1024]{2,1,0:T(8,128)(2,1)S(1)}, bf16[3,8,1024]{2,1,0:T(8,128)(2,1)S(1)}, u32[]{:S(2)}, u32[]{:S(2)}) collective-permute-start(bf16[3,8,1024]{2,1,0:T(8,128)(2,1)S(1)} %bitcast.9), channel_id=1, source_target_pairs={{0,3},{1,0},{2,1},{3,2},{4,7},{5,4},{6,5},{7,6},{8,11},{9,8},{10,9... | collective-permute-start | bytes 147464 | tf_op jit(solution)/shard_map/ppermute | solution.py:251
  18.1 4.7 %collective-permute-start.1 = (bf16[3,8,1024]{2,1,0:T(8,128)(2,1)S(1)}, bf16[3,8,1024]{2,1,0:T(8,128)(2,1)S(1)}, u32[]{:S(2)}, u32[]{:S(2)}) collective-permute-start(bf16[3,8,1024]{2,1,0:T(8,128)(2,1)S(1)} %bitcast.10), channel_id=1, source_target_pairs={{0,2},{1,3},{2,0},{3,1},{4,6},{5,7},{6,4},{7,5},{8,10},{9,11},{10,... | collective-permute-start | bytes 147464 | tf_op jit(solution)/shard_map/ppermute | solution.py:251
  18.6 4.7 %collective-permute-start = (bf16[3,8,1024]{2,1,0:T(8,128)(2,1)S(1)}, bf16[3,8,1024]{2,1,0:T(8,128)(2,1)S(1)}, u32[]{:S(2)}, u32[]{:S(2)}) collective-permute-start(bf16[3,8,1024]{2,1,0:T(8,128)(2,1)S(1)} %bitcast.11), channel_id=1, source_target_pairs={{0,1},{1,2},{2,3},{3,0},{4,5},{5,6},{6,7},{7,4},{8,9},{9,10},{10,1... | collective-permute-start | bytes 147464 | tf_op jit(solution)/shard_map/ppermute | solution.py:251
  36.7 16.4 %copy-start = (s32[96,1]{0,1:T(1,128)S(1)}, s32[96,1]{0,1:T(1,128)}, u32[]{:S(2)}) copy-start(s32[96,1]{0,1:T(1,128)} %param.6) | copy-start | bytes 1156

commit v3 on v2

--- a/solution.py
+++ b/solution.py
@@ -213,7 +213,7 @@
             acc_ref[pl.ds(pl.multiple_of((step * 4 + c) * PHASES, PHASES), PHASES), :] = totals[0] + totals[1]
         return carry
 
-    lax.fori_loop(0, STEPS, template_step, 0, unroll=4)
+    lax.fori_loop(0, STEPS, template_step, 0, unroll=True)
     for half in range(2):
         out_ref[:, half, :] = acc_ref[128 * half : 128 * half + 128, :].T[:BLOCKS]
 
@@ -222,6 +222,7 @@
     shift = lax.axis_index("sta") >> 3
     block = ((ids_ref[...] >> 5) + BLOCKS - shift) & (BLOCKS - 1)
     hot, count = routing(block)
+    narrow = ones_where(hot)
     hot = jnp.where(hot, 1.0, 0.0)
     rank = jnp.sum(hot * count, axis=0, keepdims=True)
     quarter = iota((BLOCKS, 128), 1) >> 5
@@ -233,7 +234,12 @@
         aligned = twice_ref[4 * half : 4 * half + BLOCKS, :]
         for d in range(1, 4):
             aligned = jnp.where(quarter == d, twice_ref[4 * half + d : 4 * half + d + BLOCKS, :], aligned)
-        picked = jnp.dot(aligned.T, hot, precision=lax.Precision.HIGHEST, preferred_element_type=F32)
+        aligned = aligned.T
+        high = aligned.astype(BF16)
+        rest = aligned - high.astype(F32)
+        middle = rest.astype(BF16)
+        low = (rest - middle.astype(F32)).astype(BF16)
+        picked = mm(high, narrow) + (mm(middle, narrow) + mm(low, narrow))
         picked = jnp.where(keep, picked, 0.0)
         for group in range(16):
             part = picked[8 * group : 8 * group + 8]

time: 54.3 us -> 53.7 us (0.989)
  Pallas kernels: 11.8 us -> 11.2 us
    pallas_call x1, Pallas kernels: 7.94 us -> 7.39 us  [on_device(): pl.pallas_call(correlate_kernel, out_shape=jax.ShapeDtypeStruct((BLOCKS,...]
where the time goes in v3:
time: 53.7 us; the launch traced here: 53.4 us
  starting transfers between devices  17 us (32%)
  blocking collectives  16.4 us (31%)
  Pallas kernels  11.2 us (21%)
  waiting for transfers between devices  8.83 us (16%)
    all_to_all x1, blocking collectives, on_device(): lax.all_to_all(stacks, 'sta', split_axis=0, concat_axis=0, tiled=True)  16.4 us
    all_to_all x1, starting transfers between devices, on_device(): got = lax.all_to_all(send, 'sta', split_axis=0, concat_axis=0, tiled=True)  13.3 us
    pallas_call x1, Pallas kernels, on_device(): pl.pallas_call(correlate_kernel, out_shape=jax.ShapeDtypeStruct((BLOCKS,...  7.39 us
    all_to_all x1, waiting for transfers between devices, on_device(): got = lax.all_to_all(send, 'sta', split_axis=0, concat_axis=0, tiled=True)  4.7 us
    ppermute x3, waiting for transfers between devices, on_device(): lax.ppermute(own, 'tpl', [(i, (i + hop) % OWNERS) for i in range(OWNERS)])  4.13 us
    ppermute x3, starting transfers between devices, on_device(): lax.ppermute(own, 'tpl', [(i, (i + hop) % OWNERS) for i in range(OWNERS)])  3.69 us
    pallas_call x1, Pallas kernels, on_device(): pl.pallas_call(pack_kernel, out_shape=jax.ShapeDtypeStruct((BLOCKS, 5, 4,...  2.19 us
  transfers between devices with their start and end apart: 4, of which 3 were waited for; matrix products, arithmetic and copies ran while one was open for 0% of the time, Pallas kernels for 1%

profile of v3, /device:TPU:1, one launch (start us, length us, event | category | flops | bytes accessed | tf_op | source)
XLA Modules:
  0.0 53.4 jit_solution(10387400089922063549)
XLA Ops:
  0.0 2.2 %pack.1 = bf16[64,5,4,128]{3,2,1,0:T(4,128)(2,1)} custom-call(s32[1,96]{1,0:T(1,128)} %bitcast.7, s32[3,1,96]{2,1,0:T(1,128)} %bitcast.14, bf16[3,96,256]{2,1,0:T(8,128)(2,1)} %bitcast.13), custom_call_target="tpu_custom_call" | custom-call | tf_op jit(solution)/shard_map/pack/pallas_call | solution.py:260
  2.2 0.0 copy-start.1
  2.2 13.3 %all-to-all-start = ((bf16[64,5,4,128]{3,2,1,0:T(4,128)(2,1)}), bf16[64,5,4,128]{3,2,1,0:T(4,128)(2,1)S(1)}, u32[]{:S(2)}, u32[]{:S(2)}) async-start(bf16[64,5,4,128]{3,2,1,0:T(4,128)(2,1)} %pack.1), calls=%async_computation | async-start | bytes 655360 | tf_op jit(solution)/shard_map/all_to_all | solution.py:269
  15.5 0.0 copy-done.1
  15.5 2.6 %collective-permute-start.2 = (bf16[3,8,1024]{2,1,0:T(8,128)(2,1)S(1)}, bf16[3,8,1024]{2,1,0:T(8,128)(2,1)S(1)}, u32[]{:S(2)}, u32[]{:S(2)}) collective-permute-start(bf16[3,8,1024]{2,1,0:T(8,128)(2,1)S(1)} %bitcast.9), channel_id=1, source_target_pairs={{0,3},{1,0},{2,1},{3,2},{4,7},{5,4},{6,5},{7,6},{8,11},{9,8},{10,9... | collective-permute-start | bytes 147464 | tf_op jit(solution)/shard_map/ppermute | solution.py:257
  18.1 0.5 collective-permute-start.1
  18.6 0.6 %collective-permute-start = (bf16[3,8,1024]{2,1,0:T(8,128)(2,1)S(1)}, bf16[3,8,1024]{2,1,0:T(8,128)(2,1)S(1)}, u32[]{:S(2)}, u32[]{:S(2)}) collective-permute-start(bf16[3,8,1024]{2,1,0:T(8,128)(2,1)S(1)} %bitcast.11), channel_id=1, source_target_pairs={{0,1},{1,2},{2,3},{3,0},{4,5},{5,6},{6,7},{7,4},{8,9},{9,10},{10,1... | collective-permute-start | bytes 147464 | tf_op jit(solution)/shard_map/ppermute | solution.py:257
  19.2 0.0 collective-permute-done.2.refs_3_
  19.2 3.6 %collective-permute-done.1.refs_2_ = bf16[3,8,1024]{2,1,0:T(8,128)(2,1)S(1)} collective-permute-done((bf16[3,8,1024]{2,1,0:T(8,128)(2,1)S(1)}, bf16[3,8,1024]{2,1,0:T(8,128)(2,1)S(1)}, u32[]{:S(2)}, u32[]{:S(2)}) %collective-permute-start.1) | collective-permute-done | bytes 49184 | tf_op jit(solution)/shard_map/ppermute | solution.py:257
  22.8 0.5 collective-permute-done.refs_1_
  23.3 0.7 %prepare.1.prepared_ref = f32[2,768,128]{2,1,0:T(8,128)S(1)} custom-call(bf16[3,8,1024]{2,1,0:T(8,128)(2,1)S(1)} %bitcast.12, bf16[3,8,1024]{2,1,0:T(8,128)(2,1)S(1)} %collective-permute-done.refs_1_, bf16[3,8,1024]{2,1,0:T(8,128)(2,1)S(1)} %collective-permute-done.1.refs_2_, bf16[3,8,1024]{2,1,0:T(8,128)(2,1)S(1)} %collective-permute-done.2.refs_3_), custom_call_target="tpu_custom_call" | custom-call | flops 400000000 | bytes 1048576 | tf_op jit(solution)/shard_map/prepare/pallas_call | solution.py:270
  24.0 4.7 %all-to-all-done.got_ref = bf16[64,5,4,128]{3,2,1,0:T(4,128)(2,1)S(1)} async-done(((bf16[64,5,4,128]{3,2,1,0:T(4,128)(2,1)}), bf16[64,5,4,128]{3,2,1,0:T(4,128)(2,1)S(1)}, u32[]{:S(2)}, u32[]{:S(2)}) %all-to-all-start) | async-done | bytes 327712 | tf_op jit(solution)/shard_map/all_to_all | solution.py:269
  28.7 7.4 %correlate.1 = f32[64,2,128]{2,1,0:T(2,128)S(1)} custom-call(bf16[64,5,4,128]{3,2,1,0:T(4,128)(2,1)S(1)} %all-to-all-done.got_ref, f32[2,768,128]{2,1,0:T(8,128)S(1)} %prepare.1.prepared_ref), custom_call_target="tpu_custom_call" | custom-call | tf_op jit(solution)/shard_map/correlate/pallas_call | solution.py:279
  36.1 0.0 copy-start
  36.2 16.4 %all_to_all.10.got_ref = f32[64,2,128]{2,1,0:T(2,128)S(1)} all-to-all(f32[64,2,128]{2,1,0:T(2,128)S(1)} %correlate.1), channel_id=1, replica_groups=mesh['sta'=64,'tpl'=4] {'sta'}, dimensions={0} | all-to-all | bytes 131072 | tf_op jit(solution)/shard_map/all_to_all | solution.py:298
  52.5 0.0 copy-done
  52.5 0.9 %unpack.1 = f32[8,96]{1,0:T(8,128)} custom-call(s32[1,96]{1,0:T(1,128)S(1)} %bitcast.8, f32[64,2,128]{2,1,0:T(2,128)S(1)} %all_to_all.10.got_ref), custom_call_target="tpu_custom_call" | custom-call | tf_op jit(solution)/shard_map/unpack/pallas_call | solution.py:299
Async XLA Ops:
  2.2 13.3 %copy-start.1 = (bf16[8,3,1024]{2,0,1:T(8,128)(2,1)S(1)}, bf16[8,3,1024]{2,0,1:T(8,128)(2,1)}, u32[]{:S(2)}) copy-start(bf16[8,3,1024]{2,0,1:T(8,128)(2,1)} %param.4) | copy-start | bytes 147460
  2.2 26.5 %all-to-all-start = ((bf16[64,5,4,128]{3,2,1,0:T(4,128)(2,1)}), bf16[64,5,4,128]{3,2,1,0:T(4,128)(2,1)S(1)}, u32[]{:S(2)}, u32[]{:S(2)}) async-start(bf16[64,5,4,128]{3,2,1,0:T(4,128)(2,1)} %pack.1), calls=%async_computation | async-start | bytes 655360 | tf_op jit(solution)/shard_map/all_to_all | solution.py:269
  15.5 3.7 %collective-permute-start.2 = (bf16[3,8,1024]{2,1,0:T(8,128)(2,1)S(1)}, bf16[3,8,1024]{2,1,0:T(8,128)(2,1)S(1)}, u32[]{:S(2)}, u32[]{:S(2)}) collective-permute-start(bf16[3,8,1024]{2,1,0:T(8,128)(2,1)S(1)} %bitcast.9), channel_id=1, source_target_pairs={{0,3},{1,0},{2,1},{3,2},{4,7},{5,4},{6,5},{7,6},{8,11},{9,8},{10,9... | collective-permute-start | bytes 147464 | tf_op jit(solution)/shard_map/ppermute | solution.py:257
  18.1 4.7 %collective-permute-start.1 = (bf16[3,8,1024]{2,1,0:T(8,128)(2,1)S(1)}, bf16[3,8,1024]{2,1,0:T(8,128)(2,1)S(1)}, u32[]{:S(2)}, u32[]{:S(2)}) collective-permute-start(bf16[3,8,1024]{2,1,0:T(8,128)(2,1)S(1)} %bitcast.10), channel_id=1, source_target_pairs={{0,2},{1,3},{2,0},{3,1},{4,6},{5,7},{6,4},{7,5},{8,10},{9,11},{10,... | collective-permute-start | bytes 147464 | tf_op jit(solution)/shard_map/ppermute | solution.py:257
  18.6 4.7 %collective-permute-start = (bf16[3,8,1024]{2,1,0:T(8,128)(2,1)S(1)}, bf16[3,8,1024]{2,1,0:T(8,128)(2,1)S(1)}, u32[]{:S(2)}, u32[]{:S(2)}) collective-permute-start(bf16[3,8,1024]{2,1,0:T(8,128)(2,1)S(1)} %bitcast.11), channel_id=1, source_target_pairs={{0,1},{1,2},{2,3},{3,0},{4,5},{5,6},{6,7},{7,4},{8,9},{9,10},{10,1... | collective-permute-start | bytes 147464 | tf_op jit(solution)/shard_map/ppermute | solution.py:257
  36.1 16.4 %copy-start = (s32[96,1]{0,1:T(1,128)S(1)}, s32[96,1]{0,1:T(1,128)}, u32[]{:S(2)}) copy-start(s32[96,1]{0,1:T(1,128)} %param.6) | copy-start | bytes 1156
